TPU v7x, 32 devices: a whole 2x2x4 slice. The times are simulated.
32 devices in a mesh: sta: 16 (over z, x, core), strike: 2 (over y).
Axes of the slice: x: 2, y: 2, z: 4, core: 2. Of those that a mesh axis runs over, the one named last changes fastest.
Arguments:
- data: float32 [128, 512], P('sta'), may hold values from -6 to 6
- model: float32 [64, 64, 128], P(None, 'strike'), may hold values from -6 to 6
- green: bfloat16 [16, 2, 96, 128, 128], P('sta', 'strike'), may hold values from -0.03125 to 0.03125
- block_ids: int32 [16, 2, 96], P('sta', 'strike'), may hold values from -1 to 1023, as said below
Outputs:
- residual: float32 [128, 512], P('sta')
- updated: float32 [64, 64, 128], P(None, 'strike')
Inputs may be any that keep to these rules, and one draw needn't show every extreme that they name: In each block_ids[g, h] the ids that are not -1 are distinct and stand in the first slots; every pair uses at least a third of its 96 slots, and in every draw some pair uses all 96.
All inputs are finite; a program needn't handle non-finite values.
Results may differ from a plain program's by a relative error of at most 0.0023.
Values sent between devices are 32-bit elements; how exact they have to be, the bound alone decides.
A program may use at most 64 MiB of HBM per device.

v0:
```python
import jax
import jax.numpy as jnp
from jax import lax
from jax.sharding import PartitionSpec as P

SWEEPS = 4
NU_DIFF = 0.1
STEP_LEN = 4.0


def extended(block, sides, width):
    for axis, dim in sides:
        count = lax.axis_size(axis)
        forward = [(i, i + 1) for i in range(count - 1)]
        backward = [(target, source) for source, target in forward]
        low = lax.ppermute(
            lax.slice_in_dim(block, block.shape[dim] - width, None, axis=dim), axis, forward
        )
        high = lax.ppermute(lax.slice_in_dim(block, 0, width, axis=dim), axis, backward)
        block = jnp.concatenate([low, block, high], axis=dim)
    return block


def shear_add(series):
    count_rows, windows, length = series.shape
    padded = jnp.pad(series, ((0, 0), (0, 0), (0, windows)))
    flattened = padded.reshape(count_rows, windows * (length + windows))[
        :, : windows * (length + windows - 1)
    ]
    sheared = flattened.reshape(count_rows, windows, length + windows - 1)
    return jnp.sum(sheared[:, :, :length], axis=1)


def shear_take(residual, windows):
    count_rows, length = residual.shape
    padded = jnp.pad(residual, ((0, 0), (0, windows)))
    repeated = jnp.broadcast_to(padded[:, None, :], (count_rows, windows, length + windows))
    repeated = repeated.reshape(count_rows, windows * (length + windows))
    repeated = jnp.pad(repeated, ((0, 0), (0, windows)))
    return repeated.reshape(count_rows, windows, length + windows + 1)[:, :, :length]


def laplace_step(padded, field):
    laplace = (
        padded[:, 2:, 1:-1]
        + padded[:, :-2, 1:-1]
        + padded[:, 1:-1, 2:]
        + padded[:, 1:-1, :-2]
        - 4.0 * field
    )
    return field + NU_DIFF * laplace


def local(data, model, green, block_ids):
    sta_rows, samples = data.shape
    windows, strike_rows, dip_cells = model.shape
    block = green.shape[-1]
    time_blocks = samples // block
    row_count = sta_rows * time_blocks
    blocks = green.reshape(green.shape[2:])
    slot_ids = block_ids.reshape(-1)
    usable = slot_ids >= 0
    safe_ids = jnp.where(usable, slot_ids, 0)
    row_block = safe_ids // strike_rows
    col_block = safe_ids % strike_rows
    row_target = jnp.where(usable, row_block, row_count)
    col_target = jnp.where(usable, col_block, strike_rows)
    model_bf = model.astype(jnp.bfloat16)
    columns = jnp.take(model_bf, col_block, axis=1)
    products = jnp.einsum("cts,wcs->cwt", blocks, columns, preferred_element_type=jnp.float32)
    gathered = jax.ops.segment_sum(products, row_target, num_segments=row_count)
    series = (
        gathered.reshape(sta_rows, time_blocks, windows, block)
        .transpose(0, 2, 1, 3)
        .reshape(sta_rows, windows, samples)
    )
    partial_synth = shear_add(series)
    residual = lax.psum(partial_synth, "strike") - data
    resid_bf = residual.astype(jnp.bfloat16)
    shifted = shear_take(resid_bf, windows)
    row_blocks = (
        shifted.reshape(sta_rows, windows, time_blocks, block)
        .transpose(0, 2, 1, 3)
        .reshape(row_count, windows, block)
    )
    res_rows = jnp.take(row_blocks, row_block, axis=0)
    slot_grads = jnp.einsum("cts,cwt->cws", blocks, res_rows, preferred_element_type=jnp.float32)
    per_patch = jax.ops.segment_sum(slot_grads, col_target, num_segments=strike_rows)
    partial_grad = per_patch.transpose(1, 0, 2)
    field = lax.psum(partial_grad, "sta")
    for sweep in range(SWEEPS):
        padded = extended(field, (("strike", 1),), 1)
        padded = jnp.pad(padded, ((0, 0), (0, 0), (1, 1)))
        field = laplace_step(padded, field)
    updated = model - STEP_LEN * field
    return (residual, updated)


def solution(mesh):
    in_specs = (
        P("sta", None),
        P(None, "strike", None),
        P("sta", "strike", None, None, None),
        P("sta", "strike", None),
    )
    out_specs = (P("sta", None), P(None, "strike", None))
    return jax.shard_map(local, mesh=mesh, in_specs=in_specs, out_specs=out_specs, check_vma=False)
```

profile of v0, /device:TPU:0, one launch (start us, length us, event | category | flops | bytes accessed | tf_op | source)
XLA Modules:
  0.0 228.4 jit_solution(13629013439439119440)
XLA Ops:
  7.2 0.0 copy-start
  7.2 0.0 all-reduce.9.cloned.1.call-start
  7.2 0.8 fusion.33
  8.0 0.8 compare_and_fusion
  8.8 0.7 fusion.31
  9.5 2.6 %copy.16 = bf16[64,32,128]{2,0,1:T(8,128)(2,1)} copy(f32[64,32,128]{2,1,0:T(8,128)} %param.5) | data formatting | bytes 1572864 | tf_op args[1]
  12.1 3.0 %gather_fusion = bf16[96,64,128]{2,1,0:T(8,128)(2,1)} fusion(bf16[64,32,128]{2,0,1:T(8,128)(2,1)} %copy.16, s32[1024]{0:T(1024)S(1)} %pad_clamp_fusion.1), kind=kCustom, calls=%fused_computation | custom fusion | bytes 3146112 | tf_op jit(solution)/shard_map/jit(_take)/gather | solution.py:69
  15.1 0.0 copy-done
  15.1 5.3 %fusion.2 = f32[96,64,128]{2,1,0:T(8,128)} fusion(bf16[1,1,96,128,128]{4,3,2,1,0:T(8,128)(2,1)S(1)} %copy-done, bf16[96,64,128]{2,1,0:T(8,128)(2,1)} %gather_fusion, pred[96]{0:T(512)(128)(4,1)S(1)} %compare_and_fusion.1), kind=kOutput, calls=%fused_computation.8 | convolution fusion | flops 202113024 | bytes 7864416 | tf_op jit(solution)/shard_map/cts,wcs->cwt/dot_general | solution.py:70
  20.4 1.1 broadcast.280.clone
  21.5 14.6 %scatter_fusion = f32[32,64,128]{2,1,0:T(8,128)} fusion(f32[32,64,128]{2,1,0:T(8,128)} %broadcast.280.clone, s32[96]{0:T(128)S(1)} %get-tuple-element.25, f32[96,64,128]{2,1,0:T(8,128)} %fusion.2), kind=kCustom, calls=%fused_computation.2 | custom fusion | flops 786432 | bytes 9437568 | tf_op jit(solution)/shard_map/scatter-add | solution.py:71
  36.1 1.4 copy.17
  37.4 1.2 pad.25
  38.6 2.9 %reshape.180 = f32[8,36864]{1,0:T(8,128)} reshape(f32[8,64,576]{2,1,0:T(8,128)} %pad.25) | data formatting | bytes 2359296 | tf_op jit(solution)/shard_map/reshape | solution.py:27
  41.6 0.0 copy-start.3
  41.6 3.6 %reshape.181 = f32[8,64,575]{2,1,0:T(8,128)} reshape(f32[8,36800]{1,0:T(8,128)} %bitcast.46) | data formatting | bytes 2355200 | tf_op jit(solution)/shard_map/reshape | solution.py:30
  45.1 1.3 slice_reduce_fusion
  46.5 10.1 %psum.14 = f32[8,512]{1,0:T(8,128)S(1)} all-reduce(f32[8,512]{1,0:T(8,128)S(1)} %slice_reduce_fusion), channel_id=1, replica_groups=mesh['sta'=16,'strike'=2] {'strike'}, use_global_device_ids=true, to_apply=%region_2.3 | all-reduce | flops 4096 | bytes 32768 | tf_op jit(solution)/shard_map/psum | solution.py:78
  56.6 0.0 copy-done.3
  56.6 0.6 fusion.36
  57.2 0.9 broadcast_in_dim.35
  58.1 2.7 %reshape.182 = bf16[8,36864]{1,0:T(8,128)(2,1)} reshape(bf16[8,64,576]{2,1,0:T(8,128)(2,1)} %broadcast_in_dim.35) | data formatting | bytes 1179648 | tf_op jit(solution)/shard_map/reshape | solution.py:38
  60.8 1.9 pad.27
  62.7 3.3 %reshape.183 = bf16[8,64,577]{2,1,0:T(8,128)(2,1)} reshape(bf16[8,36928]{1,0:T(8,128)(2,1)} %pad.27) | data formatting | bytes 1181696 | tf_op jit(solution)/shard_map/reshape | solution.py:40
  66.0 1.1 fusion.41
  67.1 0.8 pad_maximum_fusion.8
  68.0 3.0 %gather_fusion.1 = bf16[96,64,128]{2,1,0:T(8,128)(2,1)} fusion(bf16[32,64,128]{2,1,0:T(8,128)(2,1)} %bitcast.45, s32[1024]{0:T(1024)S(1)} %pad_clamp_fusion), kind=kCustom, calls=%fused_computation.1 | custom fusion | bytes 3146112 | tf_op jit(solution)/shard_map/jit(_take)/gather | solution.py:86
  71.0 4.0 %fusion = f32[96,64,128]{2,1,0:T(8,128)} fusion(bf16[1,1,96,128,128]{4,3,2,1,0:T(8,128)(2,1)S(1)} %copy-done, bf16[96,64,128]{2,1,0:T(8,128)(2,1)} %gather_fusion.1, pred[96]{0:T(512)(128)(4,1)S(1)} %get-tuple-element.4), kind=kOutput, calls=%fused_computation.6 | convolution fusion | flops 202113024 | bytes 7864416 | tf_op jit(solution)/shard_map/cts,cwt->cws/dot_general | solution.py:87
  75.0 1.1 broadcast.280
  76.1 14.5 %scatter_fusion.1 = f32[32,64,128]{2,1,0:T(8,128)} fusion(f32[32,64,128]{2,1,0:T(8,128)} %broadcast.280, s32[96]{0:T(128)S(1)} %get-tuple-element.23, f32[96,64,128]{2,1,0:T(8,128)} %fusion), kind=kCustom, calls=%fused_computation.3 | custom fusion | flops 786432 | bytes 9437568 | tf_op jit(solution)/shard_map/scatter-add | solution.py:88
  90.7 0.0 all-reduce.9.cloned.1.call-update
  90.7 92.7 %all-reduce.9.cloned.1.call-done = f32[64,32,128]{2,0,1:T(8,128)} async-done(((f32[64,32,128]{2,0,1:T(8,128)}), f32[64,32,128]{2,0,1:T(8,128)}) %all-reduce.9.cloned.1.call-update) | async-done | bytes 1048592 | tf_op jit(solution)/shard_map/psum | solution.py:90
  183.4 0.0 copy-start.1
  183.4 0.9 fusion.40
  184.3 1.3 collective-permute-start
  185.6 4.5 %collective-permute-start.1 = (f32[64,1,128]{2,0,1:T(8,128)S(1)}, f32[64,1,128]{2,0,1:T(8,128)S(1)}, u32[]{:S(2)}, u32[]{:S(2)}) collective-permute-start(f32[64,1,128]{2,0,1:T(8,128)S(1)} %get-tuple-element.17), channel_id=1, source_target_pairs={{0,1},{2,3},{4,5},{6,7},{8,9},{10,11},{12,13},{14,15},{16,17},{18,... | collective-permute-start | bytes 98312 | tf_op jit(solution)/shard_map/ppermute | solution.py:16
  190.1 0.0 collective-permute-done
  190.1 1.6 collective-permute-done.1
  191.7 1.9 select_maximum_fusion.6
  193.6 0.0 copy-done.1
  193.6 0.4 fusion.26
  194.0 1.3 collective-permute-start.2
  195.3 4.5 %collective-permute-start.3 = (f32[64,1,128]{2,0,1:T(8,128)S(1)}, f32[64,1,128]{2,0,1:T(8,128)S(1)}, u32[]{:S(2)}, u32[]{:S(2)}) collective-permute-start(f32[64,1,128]{2,0,1:T(8,128)S(1)} %get-tuple-element.15), channel_id=1, source_target_pairs={{0,1},{2,3},{4,5},{6,7},{8,9},{10,11},{12,13},{14,15},{16,17},{18,... | collective-permute-start | bytes 98312 | tf_op jit(solution)/shard_map/ppermute | solution.py:16
  199.8 0.0 collective-permute-done.2
  199.8 1.6 collective-permute-done.3
  201.4 0.6 select_maximum_fusion.4
  202.0 0.4 fusion.22
  202.4 1.3 collective-permute-start.4
  203.7 4.7 %collective-permute-start.5 = (f32[64,1,128]{2,0,1:T(8,128)S(1)}, f32[64,1,128]{2,0,1:T(8,128)S(1)}, u32[]{:S(2)}, u32[]{:S(2)}) collective-permute-start(f32[64,1,128]{2,0,1:T(8,128)S(1)} %get-tuple-element.13), channel_id=1, source_target_pairs={{0,1},{2,3},{4,5},{6,7},{8,9},{10,11},{12,13},{14,15},{16,17},{18,... | collective-permute-start | bytes 98312 | tf_op jit(solution)/shard_map/ppermute | solution.py:16
  208.5 0.0 collective-permute-done.4
  208.5 1.4 collective-permute-done.5
  209.9 0.6 select_maximum_fusion.2
  210.5 0.4 fusion.18
  210.9 0.0 copy-start.2
  210.9 1.4 collective-permute-start.6
  212.3 4.5 %collective-permute-start.7 = (f32[64,1,128]{2,0,1:T(8,128)S(1)}, f32[64,1,128]{2,0,1:T(8,128)S(1)}, u32[]{:S(2)}, u32[]{:S(2)}) collective-permute-start(f32[64,1,128]{2,0,1:T(8,128)S(1)} %get-tuple-element.11), channel_id=1, source_target_pairs={{0,1},{2,3},{4,5},{6,7},{8,9},{10,11},{12,13},{14,15},{16,17},{18,... | collective-permute-start | bytes 98312 | tf_op jit(solution)/shard_map/ppermute | solution.py:16
  216.9 0.0 collective-permute-done.6
  216.9 1.6 collective-permute-done.7
  218.5 0.6 select_maximum_fusion
  219.1 0.0 copy-done.2
  219.1 0.9 fusion.14
  220.0 1.6 copy.11
  (7 shorter events, 0.0 us)
Async XLA Ops:
  7.2 8.0 %copy-start = (bf16[1,1,96,128,128]{4,3,2,1,0:T(8,128)(2,1)S(1)}, bf16[1,1,96,128,128]{4,3,2,1,0:T(8,128)(2,1)}, u32[]{:S(2)}) copy-start(bf16[1,1,96,128,128]{4,3,2,1,0:T(8,128)(2,1)} %param.6) | copy-start | bytes 9437188
  7.2 176.2 %all-reduce.9.cloned.1.call-start = ((), (), s32[]{:S(2)}) async-start(), calls=%async_computation | async-start | bytes 2097152 | tf_op jit(solution)/shard_map/psum | solution.py:90
  41.6 15.1 %copy-start.3 = (f32[8,512]{1,0:T(8,128)S(1)}, f32[8,512]{1,0:T(8,128)}, u32[]{:S(2)}) copy-start(f32[8,512]{1,0:T(8,128)} %param.4) | copy-start | bytes 49156
  183.4 10.2 %copy-start.1 = (f32[64,32,128]{2,0,1:T(8,128)S(1)}, f32[64,32,128]{2,0,1:T(8,128)}, u32[]{:S(2)}) copy-start(f32[64,32,128]{2,0,1:T(8,128)} %all-reduce.9.cloned.1.call-done) | copy-start | bytes 3145732
  184.3 5.8 %collective-permute-start = (f32[64,1,128]{2,0,1:T(8,128)S(1)}, f32[64,1,128]{2,0,1:T(8,128)S(1)}, u32[]{:S(2)}, u32[]{:S(2)}) collective-permute-start(f32[64,1,128]{2,0,1:T(8,128)S(1)} %get-tuple-element.18), channel_id=1, source_target_pairs={{1,0},{3,2},{5,4},{7,6},{9,8},{11,10},{13,12},{15,14},{17,16},{19,... | collective-permute-start | bytes 98312 | tf_op jit(solution)/shard_map/ppermute | solution.py:19
  185.6 6.1 %collective-permute-start.1 = (f32[64,1,128]{2,0,1:T(8,128)S(1)}, f32[64,1,128]{2,0,1:T(8,128)S(1)}, u32[]{:S(2)}, u32[]{:S(2)}) collective-permute-start(f32[64,1,128]{2,0,1:T(8,128)S(1)} %get-tuple-element.17), channel_id=1, source_target_pairs={{0,1},{2,3},{4,5},{6,7},{8,9},{10,11},{12,13},{14,15},{16,17},{18,... | collective-permute-start | bytes 98312 | tf_op jit(solution)/shard_map/ppermute | solution.py:16
  194.0 5.9 %collective-permute-start.2 = (f32[64,1,128]{2,0,1:T(8,128)S(1)}, f32[64,1,128]{2,0,1:T(8,128)S(1)}, u32[]{:S(2)}, u32[]{:S(2)}) collective-permute-start(f32[64,1,128]{2,0,1:T(8,128)S(1)} %get-tuple-element.16), channel_id=1, source_target_pairs={{1,0},{3,2},{5,4},{7,6},{9,8},{11,10},{13,12},{15,14},{17,16},{19,... | collective-permute-start | bytes 98312 | tf_op jit(solution)/shard_map/ppermute | solution.py:19
  195.3 6.1 %collective-permute-start.3 = (f32[64,1,128]{2,0,1:T(8,128)S(1)}, f32[64,1,128]{2,0,1:T(8,128)S(1)}, u32[]{:S(2)}, u32[]{:S(2)}) collective-permute-start(f32[64,1,128]{2,0,1:T(8,128)S(1)} %get-tuple-element.15), channel_id=1, source_target_pairs={{0,1},{2,3},{4,5},{6,7},{8,9},{10,11},{12,13},{14,15},{16,17},{18,... | collective-permute-start | bytes 98312 | tf_op jit(solution)/shard_map/ppermute | solution.py:16
  202.4 6.0 %collective-permute-start.4 = (f32[64,1,128]{2,0,1:T(8,128)S(1)}, f32[64,1,128]{2,0,1:T(8,128)S(1)}, u32[]{:S(2)}, u32[]{:S(2)}) collective-permute-start(f32[64,1,128]{2,0,1:T(8,128)S(1)} %get-tuple-element.14), channel_id=1, source_target_pairs={{1,0},{3,2},{5,4},{7,6},{9,8},{11,10},{13,12},{15,14},{17,16},{19,... | collective-permute-start | bytes 98312 | tf_op jit(solution)/shard_map/ppermute | solution.py:19
  203.7 6.1 %collective-permute-start.5 = (f32[64,1,128]{2,0,1:T(8,128)S(1)}, f32[64,1,128]{2,0,1:T(8,128)S(1)}, u32[]{:S(2)}, u32[]{:S(2)}) collective-permute-start(f32[64,1,128]{2,0,1:T(8,128)S(1)} %get-tuple-element.13), channel_id=1, source_target_pairs={{0,1},{2,3},{4,5},{6,7},{8,9},{10,11},{12,13},{14,15},{16,17},{18,... | collective-permute-start | bytes 98312 | tf_op jit(solution)/shard_map/ppermute | solution.py:16
  210.9 8.2 %copy-start.2 = (f32[64,32,128]{2,1,0:T(8,128)S(1)}, f32[64,32,128]{2,1,0:T(8,128)}, u32[]{:S(2)}) copy-start(f32[64,32,128]{2,1,0:T(8,128)} %param.5) | copy-start | bytes 3145732
  210.9 6.0 %collective-permute-start.6 = (f32[64,1,128]{2,0,1:T(8,128)S(1)}, f32[64,1,128]{2,0,1:T(8,128)S(1)}, u32[]{:S(2)}, u32[]{:S(2)}) collective-permute-start(f32[64,1,128]{2,0,1:T(8,128)S(1)} %get-tuple-element.12), channel_id=1, source_target_pairs={{1,0},{3,2},{5,4},{7,6},{9,8},{11,10},{13,12},{15,14},{17,16},{19,... | collective-permute-start | bytes 98312 | tf_op jit(solution)/shard_map/ppermute | solution.py:19
  212.3 6.1 %collective-permute-start.7 = (f32[64,1,128]{2,0,1:T(8,128)S(1)}, f32[64,1,128]{2,0,1:T(8,128)S(1)}, u32[]{:S(2)}, u32[]{:S(2)}) collective-permute-start(f32[64,1,128]{2,0,1:T(8,128)S(1)} %get-tuple-element.11), channel_id=1, source_target_pairs={{0,1},{2,3},{4,5},{6,7},{8,9},{10,11},{12,13},{14,15},{16,17},{18,... | collective-permute-start | bytes 98312 | tf_op jit(solution)/shard_map/ppermute | solution.py:16
Sparse Core Ops, SparseCore 0:
  90.8 92.5 all-reduce.8
where the time goes:
time: 230 us; the launch traced here: 228 us
  waiting for transfers between devices  98.8 us (43%)
  other arithmetic  39.9 us (17%)
  local copies, waits for them, and re-layouts  32.3 us (14%)
  starting transfers between devices  23.7 us (10%)
  between operations  14.3 us (6%)
  blocking collectives  10.1 us (4%)
  matrix products  9.33 us (4%)
    psum x1, waiting for transfers between devices, local(): field = lax.psum(partial_grad, 'sta')  92.7 us
    ppermute x4, starting transfers between devices, extended(): lax.ppermute(lax.slice_in_dim(block, block.shape[dim] - width, None, axis...  18.4 us
    scatter-add x1, other arithmetic, local(): gathered = jax.ops.segment_sum(products, row_target, num_segments=row_count)  14.6 us
    scatter-add x1, other arithmetic, local(): jax.ops.segment_sum(slot_grads, col_target, num_segments=strike_rows)  14.5 us
    psum x1, blocking collectives, local(): residual = lax.psum(partial_synth, 'strike') - data  10.1 us
    ppermute x4, waiting for transfers between devices, extended(): lax.ppermute(lax.slice_in_dim(block, block.shape[dim] - width, None, axis...  6.09 us
    ppermute x4, starting transfers between devices, extended(): lax.ppermute(lax.slice_in_dim(block, 0, width, axis=dim), axis, backward)  5.29 us
    dot_general x1, matrix products, local(): jnp.einsum('cts,wcs->cwt', blocks, columns, preferred_element_type=jnp.fl...  5.28 us
  transfers between devices with their start and end apart: 9, of which 5 were waited for; matrix products, arithmetic and copies ran while one was open for 0% of the time, Pallas kernels for 0%

commit v1 on v0

--- a/solution.py
+++ b/solution.py
@@ -87,7 +87,7 @@
     slot_grads = jnp.einsum("cts,cwt->cws", blocks, res_rows, preferred_element_type=jnp.float32)
     per_patch = jax.ops.segment_sum(slot_grads, col_target, num_segments=strike_rows)
     partial_grad = per_patch.transpose(1, 0, 2)
-    field = lax.psum(partial_grad, "sta")
+    field = jnp.sum(lax.all_gather(partial_grad, "sta"), axis=0)
     for sweep in range(SWEEPS):
         padded = extended(field, (("strike", 1),), 1)
         padded = jnp.pad(padded, ((0, 0), (0, 0), (1, 1)))

time: 230 us -> 271 us (1.18)
  waiting for transfers between devices: 98.8 us -> 132 us
  other arithmetic: 39.9 us -> 48.8 us
    all_gather x0 -> x1, waiting for transfers between devices: none -> 126 us  [local(): field = jnp.sum(lax.all_gather(partial_grad, 'sta'), axis=0)]
    psum x1 -> x0, waiting for transfers between devices: 92.7 us -> none  [local(): field = lax.psum(partial_grad, 'sta')]
    reduce_sum x0 -> x1, other arithmetic: none -> 8.92 us  [local(): field = jnp.sum(lax.all_gather(partial_grad, 'sta'), axis=0)]
where the time goes in v1:
time: 271 us; the launch traced here: 270 us
  waiting for transfers between devices  132 us (49%)
  other arithmetic  48.8 us (18%)
  local copies, waits for them, and re-layouts  32.3 us (12%)
  starting transfers between devices  23.5 us (9%)
  between operations  14.3 us (5%)
  blocking collectives  10.1 us (4%)
  matrix products  9.33 us (3%)
    all_gather x1, waiting for transfers between devices, local(): field = jnp.sum(lax.all_gather(partial_grad, 'sta'), axis=0)  126 us
    ppermute x4, starting transfers between devices, extended(): lax.ppermute(lax.slice_in_dim(block, block.shape[dim] - width, None, axis...  18.2 us
    scatter-add x1, other arithmetic, local(): gathered = jax.ops.segment_sum(products, row_target, num_segments=row_count)  14.5 us
    scatter-add x1, other arithmetic, local(): jax.ops.segment_sum(slot_grads, col_target, num_segments=strike_rows)  14.5 us
    psum x1, blocking collectives, local(): residual = lax.psum(partial_synth, 'strike') - data  10.1 us
    reduce_sum x1, other arithmetic, local(): field = jnp.sum(lax.all_gather(partial_grad, 'sta'), axis=0)  8.92 us
    ppermute x4, waiting for transfers between devices, extended(): lax.ppermute(lax.slice_in_dim(block, block.shape[dim] - width, None, axis...  6.27 us
  transfers between devices with their start and end apart: 9, of which 5 were waited for; matrix products, arithmetic and copies ran while one was open for 0% of the time, Pallas kernels for 0%

profile of v1, /device:TPU:0, one launch (start us, length us, event | category | flops | bytes accessed | tf_op | source)
XLA Modules:
  0.0 270.1 jit_solution(14735303442725386322)
XLA Ops:
  7.2 0.0 copy-start
  7.2 0.0 all-gather.3.cloned.1.call-start
  7.2 0.8 fusion.33
  8.0 0.8 compare_and_fusion
  8.8 2.6 copy.19
  11.4 0.7 fusion.31
  12.1 3.0 %gather_fusion = bf16[96,64,128]{2,1,0:T(8,128)(2,1)} fusion(bf16[64,32,128]{2,0,1:T(8,128)(2,1)} %copy.19, s32[1024]{0:T(1024)S(1)} %pad_clamp_fusion.1), kind=kCustom, calls=%fused_computation | custom fusion | bytes 3146112 | tf_op jit(solution)/shard_map/jit(_take)/gather | solution.py:69
  15.1 0.0 copy-done
  15.1 5.3 %fusion.2 = f32[96,64,128]{2,1,0:T(8,128)} fusion(bf16[1,1,96,128,128]{4,3,2,1,0:T(8,128)(2,1)S(1)} %copy-done, bf16[96,64,128]{2,1,0:T(8,128)(2,1)} %gather_fusion, pred[96]{0:T(512)(128)(4,1)S(1)} %compare_and_fusion.1), kind=kOutput, calls=%fused_computation.8 | convolution fusion | flops 202113024 | bytes 7864416 | tf_op jit(solution)/shard_map/cts,wcs->cwt/dot_general | solution.py:70
  20.4 1.1 broadcast.280.clone
  21.5 14.5 %scatter_fusion = f32[32,64,128]{2,1,0:T(8,128)} fusion(f32[32,64,128]{2,1,0:T(8,128)} %broadcast.280.clone, s32[96]{0:T(128)S(1)} %get-tuple-element.25, f32[96,64,128]{2,1,0:T(8,128)} %fusion.2), kind=kCustom, calls=%fused_computation.2 | custom fusion | flops 786432 | bytes 9437568 | tf_op jit(solution)/shard_map/scatter-add | solution.py:71
  36.0 1.4 copy.20
  37.4 1.2 pad.25
  38.6 2.9 %reshape.180 = f32[8,36864]{1,0:T(8,128)} reshape(f32[8,64,576]{2,1,0:T(8,128)} %pad.25) | data formatting | bytes 2359296 | tf_op jit(solution)/shard_map/reshape | solution.py:27
  41.5 0.0 copy-start.3
  41.5 3.6 %reshape.181 = f32[8,64,575]{2,1,0:T(8,128)} reshape(f32[8,36800]{1,0:T(8,128)} %bitcast.48) | data formatting | bytes 2355200 | tf_op jit(solution)/shard_map/reshape | solution.py:30
  45.1 1.3 slice_reduce_fusion
  46.5 10.1 %psum.7 = f32[8,512]{1,0:T(8,128)S(1)} all-reduce(f32[8,512]{1,0:T(8,128)S(1)} %slice_reduce_fusion), channel_id=1, replica_groups=mesh['sta'=16,'strike'=2] {'strike'}, use_global_device_ids=true, to_apply=%region_2.3 | all-reduce | flops 4096 | bytes 32768 | tf_op jit(solution)/shard_map/psum | solution.py:78
  56.6 0.0 copy-done.3
  56.6 0.6 fusion.36
  57.2 0.9 broadcast_in_dim.35
  58.1 2.7 reshape.182
  60.8 1.9 pad.27
  62.7 3.3 %reshape.183 = bf16[8,64,577]{2,1,0:T(8,128)(2,1)} reshape(bf16[8,36928]{1,0:T(8,128)(2,1)} %pad.27) | data formatting | bytes 1181696 | tf_op jit(solution)/shard_map/reshape | solution.py:40
  66.0 1.1 fusion.41
  67.1 0.8 pad_maximum_fusion.8
  68.0 3.0 %gather_fusion.1 = bf16[96,64,128]{2,1,0:T(8,128)(2,1)} fusion(bf16[32,64,128]{2,1,0:T(8,128)(2,1)} %bitcast.47, s32[1024]{0:T(1024)S(1)} %pad_clamp_fusion), kind=kCustom, calls=%fused_computation.1 | custom fusion | bytes 3146112 | tf_op jit(solution)/shard_map/jit(_take)/gather | solution.py:86
  70.9 4.0 %fusion = f32[96,64,128]{2,1,0:T(8,128)} fusion(bf16[1,1,96,128,128]{4,3,2,1,0:T(8,128)(2,1)S(1)} %copy-done, bf16[96,64,128]{2,1,0:T(8,128)(2,1)} %gather_fusion.1, pred[96]{0:T(512)(128)(4,1)S(1)} %get-tuple-element.4), kind=kOutput, calls=%fused_computation.6 | convolution fusion | flops 202113024 | bytes 7864416 | tf_op jit(solution)/shard_map/cts,cwt->cws/dot_general | solution.py:87
  75.0 1.1 broadcast.280
  76.1 14.5 %scatter_fusion.1 = f32[32,64,128]{2,1,0:T(8,128)} fusion(f32[32,64,128]{2,1,0:T(8,128)} %broadcast.280, s32[96]{0:T(128)S(1)} %get-tuple-element.23, f32[96,64,128]{2,1,0:T(8,128)} %fusion), kind=kCustom, calls=%fused_computation.3 | custom fusion | flops 786432 | bytes 9437568 | tf_op jit(solution)/shard_map/scatter-add | solution.py:88
  90.6 0.0 all-gather.3.cloned.1.call-update
  90.7 125.5 %all-gather.3.cloned.1.call-done = f32[1024,32,128]{2,0,1:T(8,128)} async-done(((f32[64,32,128]{2,0,1:T(8,128)}), f32[1024,32,128]{2,0,1:T(8,128)}) %all-gather.3.cloned.1.call-update) | async-done | bytes 16777232 | tf_op jit(solution)/shard_map/all_gather | solution.py:90
  216.2 8.9 %reduce_sum.19 = f32[64,32,128]{2,0,1:T(8,128)} reduce(f32[16,64,32,128]{3,1,0,2:T(8,128)} %bitcast.46, f32[]{:T(128)} %constant.56.clone.1), dimensions={0}, to_apply=%region_4.5 | reduce | flops 3932160 | bytes 17825796 | tf_op jit(solution)/shard_map/reduce_sum | solution.py:90
  225.1 0.0 copy-start.1
  225.1 0.9 fusion.40
  226.0 1.3 collective-permute-start
  227.3 4.5 %collective-permute-start.1 = (f32[64,1,128]{2,0,1:T(8,128)S(1)}, f32[64,1,128]{2,0,1:T(8,128)S(1)}, u32[]{:S(2)}, u32[]{:S(2)}) collective-permute-start(f32[64,1,128]{2,0,1:T(8,128)S(1)} %get-tuple-element.17), channel_id=1, source_target_pairs={{0,1},{2,3},{4,5},{6,7},{8,9},{10,11},{12,13},{14,15},{16,17},{18,... | collective-permute-start | bytes 98312 | tf_op jit(solution)/shard_map/ppermute | solution.py:16
  231.8 0.0 collective-permute-done
  231.8 1.6 collective-permute-done.1
  233.4 1.9 select_maximum_fusion.6
  235.3 0.0 copy-done.1
  235.3 0.4 fusion.26
  235.6 1.3 collective-permute-start.2
  236.9 4.5 %collective-permute-start.3 = (f32[64,1,128]{2,0,1:T(8,128)S(1)}, f32[64,1,128]{2,0,1:T(8,128)S(1)}, u32[]{:S(2)}, u32[]{:S(2)}) collective-permute-start(f32[64,1,128]{2,0,1:T(8,128)S(1)} %get-tuple-element.15), channel_id=1, source_target_pairs={{0,1},{2,3},{4,5},{6,7},{8,9},{10,11},{12,13},{14,15},{16,17},{18,... | collective-permute-start | bytes 98312 | tf_op jit(solution)/shard_map/ppermute | solution.py:16
  241.5 0.0 collective-permute-done.2
  241.5 1.6 collective-permute-done.3
  243.1 0.6 select_maximum_fusion.4
  243.7 0.4 fusion.22
  244.1 1.3 collective-permute-start.4
  245.4 4.5 %collective-permute-start.5 = (f32[64,1,128]{2,0,1:T(8,128)S(1)}, f32[64,1,128]{2,0,1:T(8,128)S(1)}, u32[]{:S(2)}, u32[]{:S(2)}) collective-permute-start(f32[64,1,128]{2,0,1:T(8,128)S(1)} %get-tuple-element.13), channel_id=1, source_target_pairs={{0,1},{2,3},{4,5},{6,7},{8,9},{10,11},{12,13},{14,15},{16,17},{18,... | collective-permute-start | bytes 98312 | tf_op jit(solution)/shard_map/ppermute | solution.py:16
  250.0 0.0 collective-permute-done.4
  250.0 1.6 collective-permute-done.5
  251.5 0.6 select_maximum_fusion.2
  252.2 0.4 fusion.18
  252.6 0.0 copy-start.2
  252.6 1.4 collective-permute-start.6
  254.1 4.5 %collective-permute-start.7 = (f32[64,1,128]{2,0,1:T(8,128)S(1)}, f32[64,1,128]{2,0,1:T(8,128)S(1)}, u32[]{:S(2)}, u32[]{:S(2)}) collective-permute-start(f32[64,1,128]{2,0,1:T(8,128)S(1)} %get-tuple-element.11), channel_id=1, source_target_pairs={{0,1},{2,3},{4,5},{6,7},{8,9},{10,11},{12,13},{14,15},{16,17},{18,... | collective-permute-start | bytes 98312 | tf_op jit(solution)/shard_map/ppermute | solution.py:16
  258.6 0.0 collective-permute-done.6
  258.6 1.6 collective-permute-done.7
  260.2 0.6 select_maximum_fusion
  260.8 0.0 copy-done.2
  260.8 0.8 fusion.14
  261.7 1.6 copy.14
  (7 shorter events, 0.0 us)
Async XLA Ops:
  7.2 8.0 %copy-start = (bf16[1,1,96,128,128]{4,3,2,1,0:T(8,128)(2,1)S(1)}, bf16[1,1,96,128,128]{4,3,2,1,0:T(8,128)(2,1)}, u32[]{:S(2)}) copy-start(bf16[1,1,96,128,128]{4,3,2,1,0:T(8,128)(2,1)} %param.6) | copy-start | bytes 9437188
  7.2 209.0 %all-gather.3.cloned.1.call-start = ((), (), s32[]{:S(2)}) async-start(), calls=%async_computation | async-start | bytes 17825792 | tf_op jit(solution)/shard_map/all_gather | solution.py:90
  41.5 15.1 %copy-start.3 = (f32[8,512]{1,0:T(8,128)S(1)}, f32[8,512]{1,0:T(8,128)}, u32[]{:S(2)}) copy-start(f32[8,512]{1,0:T(8,128)} %param.4) | copy-start | bytes 49156
  225.1 10.2 %copy-start.1 = (f32[64,32,128]{2,0,1:T(8,128)S(1)}, f32[64,32,128]{2,0,1:T(8,128)}, u32[]{:S(2)}) copy-start(f32[64,32,128]{2,0,1:T(8,128)} %reduce_sum.19) | copy-start | bytes 3145732
  226.0 5.8 %collective-permute-start = (f32[64,1,128]{2,0,1:T(8,128)S(1)}, f32[64,1,128]{2,0,1:T(8,128)S(1)}, u32[]{:S(2)}, u32[]{:S(2)}) collective-permute-start(f32[64,1,128]{2,0,1:T(8,128)S(1)} %get-tuple-element.18), channel_id=1, source_target_pairs={{1,0},{3,2},{5,4},{7,6},{9,8},{11,10},{13,12},{15,14},{17,16},{19,... | collective-permute-start | bytes 98312 | tf_op jit(solution)/shard_map/ppermute | solution.py:19
  227.3 6.1 %collective-permute-start.1 = (f32[64,1,128]{2,0,1:T(8,128)S(1)}, f32[64,1,128]{2,0,1:T(8,128)S(1)}, u32[]{:S(2)}, u32[]{:S(2)}) collective-permute-start(f32[64,1,128]{2,0,1:T(8,128)S(1)} %get-tuple-element.17), channel_id=1, source_target_pairs={{0,1},{2,3},{4,5},{6,7},{8,9},{10,11},{12,13},{14,15},{16,17},{18,... | collective-permute-start | bytes 98312 | tf_op jit(solution)/shard_map/ppermute | solution.py:16
  235.6 5.9 %collective-permute-start.2 = (f32[64,1,128]{2,0,1:T(8,128)S(1)}, f32[64,1,128]{2,0,1:T(8,128)S(1)}, u32[]{:S(2)}, u32[]{:S(2)}) collective-permute-start(f32[64,1,128]{2,0,1:T(8,128)S(1)} %get-tuple-element.16), channel_id=1, source_target_pairs={{1,0},{3,2},{5,4},{7,6},{9,8},{11,10},{13,12},{15,14},{17,16},{19,... | collective-permute-start | bytes 98312 | tf_op jit(solution)/shard_map/ppermute | solution.py:19
  236.9 6.1 %collective-permute-start.3 = (f32[64,1,128]{2,0,1:T(8,128)S(1)}, f32[64,1,128]{2,0,1:T(8,128)S(1)}, u32[]{:S(2)}, u32[]{:S(2)}) collective-permute-start(f32[64,1,128]{2,0,1:T(8,128)S(1)} %get-tuple-element.15), channel_id=1, source_target_pairs={{0,1},{2,3},{4,5},{6,7},{8,9},{10,11},{12,13},{14,15},{16,17},{18,... | collective-permute-start | bytes 98312 | tf_op jit(solution)/shard_map/ppermute | solution.py:16
  244.1 5.9 %collective-permute-start.4 = (f32[64,1,128]{2,0,1:T(8,128)S(1)}, f32[64,1,128]{2,0,1:T(8,128)S(1)}, u32[]{:S(2)}, u32[]{:S(2)}) collective-permute-start(f32[64,1,128]{2,0,1:T(8,128)S(1)} %get-tuple-element.14), channel_id=1, source_target_pairs={{1,0},{3,2},{5,4},{7,6},{9,8},{11,10},{13,12},{15,14},{17,16},{19,... | collective-permute-start | bytes 98312 | tf_op jit(solution)/shard_map/ppermute | solution.py:19
  245.4 6.1 %collective-permute-start.5 = (f32[64,1,128]{2,0,1:T(8,128)S(1)}, f32[64,1,128]{2,0,1:T(8,128)S(1)}, u32[]{:S(2)}, u32[]{:S(2)}) collective-permute-start(f32[64,1,128]{2,0,1:T(8,128)S(1)} %get-tuple-element.13), channel_id=1, source_target_pairs={{0,1},{2,3},{4,5},{6,7},{8,9},{10,11},{12,13},{14,15},{16,17},{18,... | collective-permute-start | bytes 98312 | tf_op jit(solution)/shard_map/ppermute | solution.py:16
  252.6 8.2 %copy-start.2 = (f32[64,32,128]{2,1,0:T(8,128)S(1)}, f32[64,32,128]{2,1,0:T(8,128)}, u32[]{:S(2)}) copy-start(f32[64,32,128]{2,1,0:T(8,128)} %param.5) | copy-start | bytes 3145732
  252.6 6.0 %collective-permute-start.6 = (f32[64,1,128]{2,0,1:T(8,128)S(1)}, f32[64,1,128]{2,0,1:T(8,128)S(1)}, u32[]{:S(2)}, u32[]{:S(2)}) collective-permute-start(f32[64,1,128]{2,0,1:T(8,128)S(1)} %get-tuple-element.12), channel_id=1, source_target_pairs={{1,0},{3,2},{5,4},{7,6},{9,8},{11,10},{13,12},{15,14},{17,16},{19,... | collective-permute-start | bytes 98312 | tf_op jit(solution)/shard_map/ppermute | solution.py:19
  254.1 6.1 %collective-permute-start.7 = (f32[64,1,128]{2,0,1:T(8,128)S(1)}, f32[64,1,128]{2,0,1:T(8,128)S(1)}, u32[]{:S(2)}, u32[]{:S(2)}) collective-permute-start(f32[64,1,128]{2,0,1:T(8,128)S(1)} %get-tuple-element.11), channel_id=1, source_target_pairs={{0,1},{2,3},{4,5},{6,7},{8,9},{10,11},{12,13},{14,15},{16,17},{18,... | collective-permute-start | bytes 98312 | tf_op jit(solution)/shard_map/ppermute | solution.py:16
Sparse Core Ops, SparseCore 0:
  90.8 125.3 all-gather.2
